TPU v7x, 256 devices: a whole 4x4x8 slice. The times are simulated.
256 devices in a mesh: section: 2 (over x_hi), fsdp: 64 (over y, z, x_lo), dp: 2 (over core).
Axes of the slice: x: 4 (x_hi: 2, x_lo: 2; x = x_hi * 2 + x_lo), y: 4, z: 8, core: 2. Of those that a mesh axis runs over, the one named last changes fastest.
Arguments:
- hidden: bfloat16 [4, 512, 8192], P(('section', 'dp'), 'fsdp'), may hold values from -7 to 7
- cotangent: bfloat16 [4, 512, 8192], P(('section', 'dp'), None, 'fsdp'), may hold values from -6 to 6
- seg_ids: int32 [4, 512], P(('section', 'dp')), may hold values from 0 to 8, as said below
- advantage: float32 [4, 8], P(('section', 'dp')), may hold values from -4 to 4
- w_query: bfloat16 [8192, 8192], P('fsdp'), may hold values from -6 to 6
- w_key: bfloat16 [8192, 1024], P('fsdp'), may hold values from -6 to 6
- w_value: bfloat16 [8192, 1024], P('fsdp'), may hold values from -6 to 6
Outputs:
- rollout_query: bfloat16 [8192, 8192], P(None, 'fsdp')
- rollout_key: bfloat16 [8192, 8192], P(None, 'fsdp')
- rollout_value: bfloat16 [8192, 8192], P(None, 'fsdp')
Inputs may be any that keep to these rules, and one draw needn't show every extreme that they name: `seg_ids`: in each block ids never fall; each id below 8 covers 1 to 64 positions, one of them exactly 64, and every id below 8 appears; id 8 marks padding at the block's end.
All inputs are finite; a program needn't handle non-finite values.
Results may differ from a plain program's by a relative error of at most 0.015.
The roundings to bfloat16 on the way count: a program that leaves them out, or rounds other values in their place, can miss the bound.
Values may be sent and summed in bfloat16 or wider, within the bound.
No kernel may reach another device: no remote copies, remote signals or barrier semaphores. Data moves between devices by JAX's collectives and lax.ppermute only.
A program may use at most 64 MiB of HBM per device.

v0:
```python
import jax
import jax.numpy as jnp
from jax import lax
from jax.sharding import Mesh, PartitionSpec as P

D = 8192
HD = 128
RESP = 8
step_rate = 200.0
rope_base = 1000000.0
norm_eps = 1e-06
masked_score = -1e30
YZ = ("y", "zh", "zl")
KH = ("y", "zh")
MEM = ("zl", "core")
X = ("xh", "xl")
FS = ("y", "zh", "zl", "xl")


def rotate(field, cosine_table, sine_table):
    half_width = field.shape[-1] // 2
    lead_half = field[..., :half_width]
    tail_half = field[..., half_width:]
    return jnp.concatenate(
        [
            lead_half * cosine_table - tail_half * sine_table,
            tail_half * cosine_table + lead_half * sine_table,
        ],
        -1,
    )


def angles(seg_row):
    span_count = seg_row.shape[0]
    earlier = jnp.sum((seg_row[None, :] < seg_row[:, None]).astype(jnp.int32), axis=1)
    positions = jnp.arange(span_count, dtype=jnp.int32) - earlier
    frequency = rope_base ** (-jnp.arange(HD // 2, dtype=jnp.float32) * 2.0 / HD)
    phase_grid = positions.astype(jnp.float32)[:, None] * frequency[None, :]
    return (jnp.cos(phase_grid), jnp.sin(phase_grid))


def token_weights(seg_row, advantage_row):
    id_range = jnp.arange(RESP + 1, dtype=jnp.int32)
    onehot = (seg_row[:, None] == id_range[None, :]).astype(jnp.float32)
    counts = jnp.sum(onehot, axis=0)[:RESP]
    per_token = -advantage_row / counts
    return jnp.sum(onehot[:, :RESP] * per_token[None, :], axis=1)


def attend_back(q_rot, k_rot, v_bf, grad_context, allowed):
    score_scale = HD ** (-0.5)
    f32 = jnp.float32
    scores = jnp.einsum("td,ud->tu", q_rot, k_rot, preferred_element_type=f32) * score_scale
    scores = jnp.where(allowed, scores, masked_score)
    row_top = jnp.max(scores, axis=-1, keepdims=True)
    exponent = jnp.exp(scores - row_top)
    attention = exponent / jnp.sum(exponent, axis=-1, keepdims=True)
    attention_bf = attention.astype(jnp.bfloat16)
    grad_prob = jnp.einsum("td,ud->tu", grad_context, v_bf, preferred_element_type=f32)
    inner_sum = jnp.sum(attention * grad_prob, axis=-1, keepdims=True)
    dscore = (attention * (grad_prob - inner_sum)).astype(jnp.bfloat16)
    grad_query = jnp.einsum("tu,ud->td", dscore, k_rot, preferred_element_type=f32) * score_scale
    grad_key = jnp.einsum("tu,td->ud", dscore, q_rot, preferred_element_type=f32) * score_scale
    grad_value = jnp.einsum("tu,td->ud", attention_bf, grad_context, preferred_element_type=f32)
    return (grad_query, grad_key, grad_value)


def swap(x):
    return lax.ppermute(x, ("xl", "core"), [(0, 0), (1, 2), (2, 1), (3, 3)])


def flip(x, axes):
    n = 2 ** len(axes)
    return lax.ppermute(x, axes, [(i, n - 1 - i) for i in range(n)])


def exchange(x, axes):
    return lax.all_to_all(x, axes, split_axis=0, concat_axis=0, tiled=True)


def spread(x, axes):
    n = lax.axis_size(axes)
    return exchange(jnp.broadcast_to(x[None], (n,) + x.shape), axes)


def ordered(mine, other, bit):
    first = jnp.where(bit == 0, mine, other)
    second = jnp.where(bit == 0, other, mine)
    return (first, second)


def local(hidden, cotangent, seg_ids, advantage, w_query, w_key, w_value):
    f32 = jnp.float32
    bf16 = jnp.bfloat16
    inv_width = D ** (-0.5)
    xh = lax.axis_index("xh")
    xl = lax.axis_index("xl")
    core = lax.axis_index("core")
    zl = lax.axis_index("zl")
    member = zl * 2 + core
    ring = xh * 2 + xl
    token_rows = hidden[0].astype(f32)
    normed_own = (
        token_rows * lax.rsqrt(jnp.mean(token_rows * token_rows, axis=-1, keepdims=True) + norm_eps)
    ).astype(bf16)
    normed_own = swap(normed_own)
    cot = swap(cotangent[0])
    seg_row = swap(seg_ids[0])
    adv_row = swap(advantage[0])
    normed = lax.all_gather(normed_own, YZ + ("core",), axis=0, tiled=True)
    block_len = normed.shape[0]
    wq = w_query.reshape(2, 64, 32, 2, HD)
    wq = lax.dynamic_index_in_dim(wq, xh, 0, keepdims=False)
    wq = lax.dynamic_index_in_dim(wq, core, 2, keepdims=False)
    wq = exchange(wq.transpose(1, 0, 2), YZ)
    wq_l = flip(wq, ("xl",))
    wq_h = flip(wq, ("xh",))
    wq_b = flip(wq, X)
    mine = ordered(wq, wq_l, xl)
    theirs = ordered(wq_h, wq_b, xl)
    row0 = ordered(mine[0], theirs[0], xh)
    row1 = ordered(mine[1], theirs[1], xh)
    q_cols = jnp.stack([row0[0], row0[1], row1[0], row1[1]], axis=1).reshape(D, HD)
    wkv = jnp.concatenate([w_key.reshape(128, 8, HD), w_value.reshape(128, 8, HD)], axis=-1)
    wkv = swap(exchange(wkv.transpose(1, 0, 2), KH))
    cosine_table, sine_table = angles(seg_row)
    weight_row = token_weights(seg_row, adv_row)
    grad_context = (cot.astype(f32) * weight_row[:, None]).astype(bf16)
    place = jnp.arange(block_len, dtype=jnp.int32)
    allowed = (seg_row[:, None] == seg_row[None, :]) & (place[None, :] <= place[:, None])
    normed_m = lax.dynamic_index_in_dim(
        normed.reshape(block_len, 8, 8, HD), member, 2, keepdims=False
    ).reshape(block_len, 1024)
    kv_part = jnp.dot(normed_m, wkv.reshape(1024, 2 * HD), preferred_element_type=f32)
    kv_own = jnp.sum(exchange(kv_part.reshape(8, 64, 2 * HD), MEM), axis=0) * inv_width
    cos_own = lax.dynamic_slice_in_dim(cosine_table, member * 64, 64)
    sin_own = lax.dynamic_slice_in_dim(sine_table, member * 64, 64)
    kv_own = jnp.concatenate([rotate(kv_own[:, :HD], cos_own, sin_own), kv_own[:, HD:]], -1).astype(
        bf16
    )
    kv = spread(kv_own, MEM).reshape(block_len, 2 * HD)
    queries = jnp.dot(normed, q_cols, preferred_element_type=f32) * inv_width
    q_rot = rotate(queries, cosine_table, sine_table).astype(bf16)
    grad_query, grad_key, grad_value = attend_back(
        q_rot, kv[:, :HD], kv[:, HD:], grad_context, allowed
    )
    scaled_q = (rotate(grad_query, cosine_table, -sine_table) * inv_width).astype(bf16)
    scaled_kv = (
        jnp.concatenate([rotate(grad_key, cosine_table, -sine_table), grad_value], -1) * inv_width
    ).astype(bf16)
    kv_sum = exchange(scaled_kv.reshape(8, 64, 2 * HD), MEM).astype(f32)
    kv_sum = jnp.sum(kv_sum, axis=0).astype(bf16)
    kv_sum = spread(kv_sum, MEM).reshape(block_len, 2 * HD)
    contract = (((0,), (0,)), ((), ()))
    part_q = lax.dot_general(normed, scaled_q, contract, preferred_element_type=f32).astype(bf16)
    part_q = exchange(part_q.reshape(4, 2048, HD), X).astype(f32)
    old_q = lax.dynamic_slice_in_dim(q_cols, ring * 2048, 2048)
    new_q = (old_q.astype(f32) - step_rate * jnp.sum(part_q, axis=0)).astype(bf16)
    near = swap(new_q)
    far = lax.ppermute(
        new_q,
        ("xh", "xl", "core"),
        [
            (h * 4 + l * 2 + c, (1 - h) * 4 + c * 2 + l)
            for h in (0, 1)
            for l in (0, 1)
            for c in (0, 1)
        ],
    )
    near_c = flip(near, ("core",))
    far_c = flip(far, ("core",))
    near = ordered(near, near_c, core)
    far = ordered(far, far_c, core)
    low = ordered(near[0], far[0], xh)
    high = ordered(near[1], far[1], xh)
    roll_q = jnp.stack([low[0], high[0], low[1], high[1]], axis=0).reshape(D, HD)
    part_kv = lax.dot_general(normed_m, kv_sum, contract, preferred_element_type=f32).astype(bf16)
    part_kv = exchange(part_kv.reshape(4, 256, 2 * HD), X).astype(f32)
    old_kv = lax.dynamic_slice_in_dim(wkv, ring * 2, 2).reshape(256, 2 * HD)
    new_kv = (old_kv.astype(f32) - step_rate * jnp.sum(part_kv, axis=0)).astype(bf16)
    new_kv = spread(new_kv, ("zl",))
    new_kv = spread(new_kv, X)
    other = flip(new_kv, ("core",))
    new_kv = jnp.stack(ordered(new_kv, other, core), axis=0)
    new_kv = new_kv.reshape(2, 4, 4, 2, 128, 2 * HD).transpose(1, 3, 2, 0, 4, 5).reshape(D, 2 * HD)
    return (roll_q, new_kv[:, :HD], new_kv[:, HD:])


def solution(mesh):
    grid = Mesh(mesh.devices.reshape(2, 4, 2, 4, 2, 2), ("xh", "y", "zh", "zl", "xl", "core"))
    groups = ("xh", "core")
    in_specs = (
        P(groups, FS, None),
        P(groups, None, FS),
        P(groups, None),
        P(groups, None),
        P(FS, None),
        P(FS, None),
        P(FS, None),
    )
    out_specs = (P(None, FS), P(None, FS), P(None, FS))
    return jax.shard_map(local, mesh=grid, in_specs=in_specs, out_specs=out_specs, check_vma=False)
```

profile of v0, /device:TPU:1, one launch (start us, length us, event | category | flops | bytes accessed | tf_op | source)
XLA Modules:
  0.0 324.4 jit_solution(6756234446904016995)
XLA Ops:
  9.4 4.5 %collective-permute-start.3 = (bf16[8,8192]{1,0:T(8,128)(2,1)S(1)}, bf16[8,8192]{1,0:T(8,128)(2,1)S(1)}, u32[]{:S(2)}, u32[]{:S(2)}) collective-permute-start(bf16[8,8192]{1,0:T(8,128)(2,1)S(1)} %fusion.11), channel_id=1, source_target_pairs={{0,0},{1,2},{2,1},{3,3},{4,4},{5,6},{6,5},{7,7},{8,8},{9,10},{10,9... | collective-permute-start | bytes 393224 | tf_op jit(solution)/shard_map/ppermute | solution.py:69
  13.9 2.6 collective-permute-done.3
  17.2 3.2 reshape.127
  21.7 1.4 copy.73
  23.1 11.3 %all-to-all-start = ((bf16[32,64,128]{2,1,0:T(8,128)(2,1)}), bf16[32,64,128]{2,1,0:T(8,128)(2,1)S(1)}, u32[]{:S(2)}, u32[]{:S(2)}) async-start(bf16[32,64,128]{2,1,0:T(8,128)(2,1)} %bitcast.87), calls=%async_computation | async-start | bytes 1048576 | tf_op jit(solution)/shard_map/all_to_all | solution.py:78
  35.4 14.5 %all-to-all-done = bf16[32,64,128]{2,1,0:T(8,128)(2,1)S(1)} async-done(((bf16[32,64,128]{2,1,0:T(8,128)(2,1)}), bf16[32,64,128]{2,1,0:T(8,128)(2,1)S(1)}, u32[]{:S(2)}, u32[]{:S(2)}) %all-to-all-start) | async-done | bytes 524320 | tf_op jit(solution)/shard_map/all_to_all | solution.py:78
  50.0 4.4 %all-to-all-start.1 = ((bf16[8,128,256]{2,1,0:T(8,128)(2,1)}), bf16[8,128,256]{2,1,0:T(8,128)(2,1)}, u32[]{:S(2)}, u32[]{:S(2)}) async-start(bf16[8,128,256]{2,1,0:T(8,128)(2,1)} %maximum_bitcast_fusion.1), calls=%async_computation.1 | async-start | bytes 1048576 | tf_op jit(solution)/shard_map/all_to_all | solution.py:78
  54.4 3.5 %collective-permute-start.4 = (s32[512]{0:T(512)S(1)}, s32[512]{0:T(512)S(1)}, u32[]{:S(2)}, u32[]{:S(2)}) collective-permute-start(s32[512]{0:T(512)S(1)} %bitcast.106), channel_id=1, source_target_pairs={{0,0},{1,2},{2,1},{3,3},{4,4},{5,6},{6,5},{7,7},{8,8},{9,10},{10,9... | collective-permute-start | bytes 6152 | tf_op jit(solution)/shard_map/ppermute | solution.py:69
  57.9 2.1 collective-permute-start.7
  60.0 2.8 collective-permute-start.1
  63.9 3.1 collective-permute-start.6
  67.4 4.1 %all-to-all-done.1 = bf16[8,128,256]{2,1,0:T(8,128)(2,1)} async-done(((bf16[8,128,256]{2,1,0:T(8,128)(2,1)}), bf16[8,128,256]{2,1,0:T(8,128)(2,1)}, u32[]{:S(2)}, u32[]{:S(2)}) %all-to-all-start.1) | async-done | bytes 524320 | tf_op jit(solution)/shard_map/all_to_all | solution.py:78
  71.5 2.1 collective-permute-done
  73.5 4.8 %collective-permute-start.5 = (bf16[8,128,256]{2,1,0:T(8,128)(2,1)}, bf16[8,128,256]{2,1,0:T(8,128)(2,1)S(1)}, u32[]{:S(2)}, u32[]{:S(2)}) collective-permute-start(bf16[8,128,256]{2,1,0:T(8,128)(2,1)} %all-to-all-done.1), channel_id=1, source_target_pairs={{0,0},{1,2},{2,1},{3,3},{4,4},{5,6},{6,5},{7,7},{8,8},{9,10},{10,9... | collective-permute-start | bytes 1572872 | tf_op jit(solution)/shard_map/ppermute | solution.py:69
  78.3 6.2 %collective-permute-done.1 = bf16[32,64,128]{2,1,0:T(8,128)(2,1)S(1)} collective-permute-done((bf16[32,64,128]{2,1,0:T(8,128)(2,1)S(1)}, bf16[32,64,128]{2,1,0:T(8,128)(2,1)S(1)}, u32[]{:S(2)}, u32[]{:S(2)}) %collective-permute-start.1) | collective-permute-done | bytes 524320 | tf_op jit(solution)/shard_map/ppermute | solution.py:74
  85.7 1.6 select_bitcast_fusion.7
  87.3 24.6 %all-gather.2.cloned.1.call-done = bf16[512,8192]{1,0:T(8,128)(2,1)} async-done(((bf16[8,8192]{1,0:T(8,128)(2,1)}), bf16[512,8192]{1,0:T(8,128)(2,1)}) %all-gather.2.cloned.1.call-update) | async-done | bytes 8388624 | tf_op jit(solution)/shard_map/all_gather | solution.py:110
  111.9 9.3 %copy.64 = bf16[64,8,64,128]{3,2,1,0:T(8,128)(2,1)} copy(bf16[64,8,64,128]{3,1,2,0:T(8,128)(2,1)} %bitcast.88) | data formatting | bytes 16777216
  121.2 5.6 %constant_dynamic-slice_fusion.1 = bf16[512,8,1,128]{3,2,1,0:T(2,128)(2,1)S(1)} fusion(bf16[512,8,8,128]{3,2,1,0:T(8,128)(2,1)} %bitcast.90, s32[]{:T(128)S(6)} %select_n.135), kind=kLoop, calls=%fused_computation.100 | loop fusion | bytes 2097156 | tf_op jit(solution)/shard_map/jit(dynamic_index_in_dim)/dynamic_slice | solution.py:131
  128.7 4.3 %all-to-all-start.2 = ((f32[8,64,256]{2,1,0:T(8,128)}), f32[8,64,256]{2,1,0:T(8,128)}, u32[]{:S(2)}, u32[]{:S(2)}) async-start(f32[8,64,256]{2,1,0:T(8,128)} %fusion.50), calls=%async_computation.2 | async-start | bytes 1048576 | tf_op jit(solution)/shard_map/all_to_all | solution.py:78
  133.0 1.8 pad_maximum_fusion
  134.8 6.3 %convolution_multiply_fusion.3 = f32[512,128]{0,1:T(8,128)S(1)} fusion(bf16[512,8192]{1,0:T(8,128)(2,1)} %all-gather.2.cloned.1.call-done, bf16[8192,128]{1,0:T(8,128)(2,1)S(1)} %bitcast.91), kind=kOutput, calls=%fused_computation.11 | convolution fusion | flops 1073807360 | bytes 10747904 | tf_op jit(solution)/shard_map/dot_general | solution.py:142
  142.3 5.2 %all-to-all-done.2 = f32[8,64,256]{2,1,0:T(8,128)} async-done(((f32[8,64,256]{2,1,0:T(8,128)}), f32[8,64,256]{2,1,0:T(8,128)}, u32[]{:S(2)}, u32[]{:S(2)}) %all-to-all-start.2) | async-done | bytes 524320 | tf_op jit(solution)/shard_map/all_to_all | solution.py:78
  150.4 4.3 %all-to-all-start.3 = ((bf16[8,64,256]{2,1,0:T(8,128)(2,1)}), bf16[8,64,256]{2,1,0:T(8,128)(2,1)S(1)}, u32[]{:S(2)}, u32[]{:S(2)}) async-start(bf16[8,64,256]{2,1,0:T(8,128)(2,1)} %broadcast_in_dim.11), calls=%async_computation.3 | async-start | bytes 524288 | tf_op jit(solution)/shard_map/all_to_all | solution.py:78
  156.0 7.4 %all-to-all-done.3 = bf16[8,64,256]{2,1,0:T(8,128)(2,1)S(1)} async-done(((bf16[8,64,256]{2,1,0:T(8,128)(2,1)}), bf16[8,64,256]{2,1,0:T(8,128)(2,1)S(1)}, u32[]{:S(2)}, u32[]{:S(2)}) %all-to-all-start.3) | async-done | bytes 262176 | tf_op jit(solution)/shard_map/all_to_all | solution.py:78
  164.1 1.4 multiply_reduce_fusion
  167.1 1.3 fusion.29
  169.4 1.7 copy.58
  171.1 1.8 fusion.8
  173.2 12.1 %all_to_all.50 = bf16[8,64,256]{2,1,0:T(8,128)(2,1)S(1)} all-to-all(bf16[8,64,256]{2,1,0:T(8,128)(2,1)S(1)} %fusion.7), channel_id=1, replica_groups=mesh['xh'=2,'y'=4,'zh'=2,'zl'=4,'xl'=2,'core'=2] {'zl','core'}, dimensions={0} | all-to-all | bytes 524288 | tf_op jit(solution)/shard_map/all_to_all | solution.py:78
  186.7 12.1 %all_to_all.51 = bf16[8,64,256]{2,1,0:T(8,128)(2,1)S(1)} all-to-all(bf16[8,64,256]{2,1,0:T(8,128)(2,1)S(1)} %broadcast_in_dim.13), channel_id=1, replica_groups=mesh['xh'=2,'y'=4,'zh'=2,'zl'=4,'xl'=2,'core'=2] {'zl','core'}, dimensions={0} | all-to-all | bytes 524288 | tf_op jit(solution)/shard_map/all_to_all | solution.py:78
  198.9 1.3 convolution_convert_fusion.1
  200.2 4.0 %all-to-all-start.7 = ((bf16[4,256,256]{2,1,0:T(8,128)(2,1)}), bf16[4,256,256]{2,1,0:T(8,128)(2,1)S(1)}, u32[]{:S(2)}, u32[]{:S(2)}) async-start(bf16[4,256,256]{2,1,0:T(8,128)(2,1)} %bitcast.103), calls=%async_computation.7 | async-start | bytes 1048576 | tf_op jit(solution)/shard_map/all_to_all | solution.py:78
  204.1 7.1 %convolution_convert_fusion = bf16[8192,128]{1,0:T(8,128)(2,1)} fusion(bf16[512,8192]{1,0:T(8,128)(2,1)} %all-gather.2.cloned.1.call-done, f32[512,64]{0,1:T(8,128)S(1)} %get-tuple-element.23, f32[512,64]{0,1:T(8,128)S(1)} %copy-done.7), kind=kOutput, calls=%fused_computation | convolution fusion | flops 1074987008 | bytes 10747904 | tf_op jit(solution)/shard_map/dot_general | solution.py:155
  212.1 4.5 %all-to-all-start.4 = ((bf16[4,2048,128]{2,1,0:T(8,128)(2,1)}), bf16[4,2048,128]{2,1,0:T(8,128)(2,1)}, u32[]{:S(2)}, u32[]{:S(2)}) async-start(bf16[4,2048,128]{2,1,0:T(8,128)(2,1)} %bitcast.18), calls=%async_computation.4 | async-start | bytes 4194304 | tf_op jit(solution)/shard_map/all_to_all | solution.py:78
  217.6 23.0 %all-to-all-done.4 = bf16[4,2048,128]{2,1,0:T(8,128)(2,1)} async-done(((bf16[4,2048,128]{2,1,0:T(8,128)(2,1)}), bf16[4,2048,128]{2,1,0:T(8,128)(2,1)}, u32[]{:S(2)}, u32[]{:S(2)}) %all-to-all-start.4) | async-done | bytes 2097184 | tf_op jit(solution)/shard_map/all_to_all | solution.py:78
  240.6 17.9 %all_to_all.52 = bf16[4,256,256]{2,1,0:T(8,128)(2,1)S(1)} all-to-all(bf16[4,256,256]{2,1,0:T(8,128)(2,1)S(1)} %broadcast_in_dim.14), channel_id=1, replica_groups=mesh['xh'=2,'y'=4,'zh'=2,'zl'=4,'xl'=2,'core'=2] {'zl'}, dimensions={0} | all-to-all | bytes 1048576 | tf_op jit(solution)/shard_map/all_to_all | solution.py:78
  258.5 1.5 broadcast_in_dim.15
  260.0 4.4 %all-to-all-start.9 = ((bf16[4,4,256,256]{3,2,1,0:T(8,128)(2,1)}), bf16[4,4,256,256]{3,2,1,0:T(8,128)(2,1)}, u32[]{:S(2)}, u32[]{:S(2)}) async-start(bf16[4,4,256,256]{3,2,1,0:T(8,128)(2,1)} %broadcast_in_dim.15), calls=%async_computation.9 | async-start | bytes 4194304 | tf_op jit(solution)/shard_map/all_to_all | solution.py:78
  264.5 2.0 convert_reduce_fusion
  266.5 22.5 %all-to-all-done.9 = bf16[4,4,256,256]{3,2,1,0:T(8,128)(2,1)} async-done(((bf16[4,4,256,256]{3,2,1,0:T(8,128)(2,1)}), bf16[4,4,256,256]{3,2,1,0:T(8,128)(2,1)}, u32[]{:S(2)}, u32[]{:S(2)}) %all-to-all-start.9) | async-done | bytes 2097184 | tf_op jit(solution)/shard_map/all_to_all | solution.py:78
  289.0 2.9 collective-permute-start.12
  292.8 2.1 collective-permute-start.8
  295.0 12.5 %collective-permute-done.10 = bf16[2048,128]{1,0:T(8,128)(2,1)S(1)} collective-permute-done((bf16[2048,128]{1,0:T(8,128)(2,1)S(1)}, bf16[2048,128]{1,0:T(8,128)(2,1)S(1)}, u32[]{:S(2)}, u32[]{:S(2)}) %collective-permute-start.10) | collective-permute-done | bytes 524320 | tf_op jit(solution)/shard_map/ppermute | solution.py:160
  308.0 1.4 collective-permute-done.11
  310.3 1.6 pad_maximum_fusion.1
  311.9 2.5 broadcast_select_fusion.1
  315.3 2.3 fusion.49
  (86 shorter events, 25.1 us)
Async XLA Ops:
  7.2 27.3 %copy-start = (bf16[128,1024]{1,0:T(8,128)(2,1)S(1)}, bf16[128,1024]{1,0:T(8,128)(2,1)}, u32[]{:S(2)}) copy-start(bf16[128,1024]{1,0:T(8,128)(2,1)} %param.12) | copy-start | bytes 786436
  7.2 104.7 %all-gather.2.cloned.1.call-start = ((), (), s32[]{:S(2)}) async-start(), calls=%async_computation.10 | async-start | bytes 8519680 | tf_op jit(solution)/shard_map/all_gather | solution.py:110
  9.4 7.1 %collective-permute-start.3 = (bf16[8,8192]{1,0:T(8,128)(2,1)S(1)}, bf16[8,8192]{1,0:T(8,128)(2,1)S(1)}, u32[]{:S(2)}, u32[]{:S(2)}) collective-permute-start(bf16[8,8192]{1,0:T(8,128)(2,1)S(1)} %fusion.11), channel_id=1, source_target_pairs={{0,0},{1,2},{2,1},{3,3},{4,4},{5,6},{6,5},{7,7},{8,8},{9,10},{10,9... | collective-permute-start | bytes 393224 | tf_op jit(solution)/shard_map/ppermute | solution.py:69
  16.5 0.7 copy-start.9
  20.4 14.0 %copy-start.8 = (bf16[128,1024]{1,0:T(8,128)(2,1)S(1)}, bf16[128,1024]{1,0:T(8,128)(2,1)}, u32[]{:S(2)}) copy-start(bf16[128,1024]{1,0:T(8,128)(2,1)} %param.13) | copy-start | bytes 786436
  23.1 31.3 %copy-start.13 = (s32[1,512]{1,0:T(1,128)S(1)}, s32[1,512]{1,0:T(1,128)}, u32[]{:S(2)}) copy-start(s32[1,512]{1,0:T(1,128)} %param.9) | copy-start | bytes 6148
  23.1 26.9 %all-to-all-start = ((bf16[32,64,128]{2,1,0:T(8,128)(2,1)}), bf16[32,64,128]{2,1,0:T(8,128)(2,1)S(1)}, u32[]{:S(2)}, u32[]{:S(2)}) async-start(bf16[32,64,128]{2,1,0:T(8,128)(2,1)} %bitcast.87), calls=%async_computation | async-start | bytes 1048576 | tf_op jit(solution)/shard_map/all_to_all | solution.py:78
  50.0 21.5 %all-to-all-start.1 = ((bf16[8,128,256]{2,1,0:T(8,128)(2,1)}), bf16[8,128,256]{2,1,0:T(8,128)(2,1)}, u32[]{:S(2)}, u32[]{:S(2)}) async-start(bf16[8,128,256]{2,1,0:T(8,128)(2,1)} %maximum_bitcast_fusion.1), calls=%async_computation.1 | async-start | bytes 1048576 | tf_op jit(solution)/shard_map/all_to_all | solution.py:78
  54.4 9.6 %collective-permute-start.4 = (s32[512]{0:T(512)S(1)}, s32[512]{0:T(512)S(1)}, u32[]{:S(2)}, u32[]{:S(2)}) collective-permute-start(s32[512]{0:T(512)S(1)} %bitcast.106), channel_id=1, source_target_pairs={{0,0},{1,2},{2,1},{3,3},{4,4},{5,6},{6,5},{7,7},{8,8},{9,10},{10,9... | collective-permute-start | bytes 6152 | tf_op jit(solution)/shard_map/ppermute | solution.py:69
  57.9 96.8 %collective-permute-start.7 = (f32[8]{0:T(128)}, f32[8]{0:T(128)}, u32[]{:S(2)}, u32[]{:S(2)}) collective-permute-start(f32[8]{0:T(128)} %bitcast.17), channel_id=1, source_target_pairs={{0,0},{1,2},{2,1},{3,3},{4,4},{5,6},{6,5},{7,7},{8,8},{9,10},{10,9... | collective-permute-start | bytes 104 | tf_op jit(solution)/shard_map/ppermute | solution.py:69
  59.9 13.6 %collective-permute-start = (bf16[32,64,128]{2,1,0:T(8,128)(2,1)S(1)}, bf16[32,64,128]{2,1,0:T(8,128)(2,1)S(1)}, u32[]{:S(2)}, u32[]{:S(2)}) collective-permute-start(bf16[32,64,128]{2,1,0:T(8,128)(2,1)S(1)} %all-to-all-done), channel_id=1, source_target_pairs={{0,2},{2,0},{1,3},{3,1},{4,6},{6,4},{5,7},{7,5},{8,10},{10,8},{9,1... | collective-permute-start | bytes 1572872 | tf_op jit(solution)/shard_map/ppermute | solution.py:74
  60.0 24.5 %collective-permute-start.1 = (bf16[32,64,128]{2,1,0:T(8,128)(2,1)S(1)}, bf16[32,64,128]{2,1,0:T(8,128)(2,1)S(1)}, u32[]{:S(2)}, u32[]{:S(2)}) collective-permute-start(bf16[32,64,128]{2,1,0:T(8,128)(2,1)S(1)} %all-to-all-done), channel_id=1, source_target_pairs={{0,128},{128,0},{1,129},{129,1},{2,130},{130,2},{3,131},{131,3},{4... | collective-permute-start | bytes 1572872 | tf_op jit(solution)/shard_map/ppermute | solution.py:74
  62.8 22.9 %collective-permute-start.2 = (bf16[32,64,128]{2,1,0:T(8,128)(2,1)S(1)}, bf16[32,64,128]{2,1,0:T(8,128)(2,1)S(1)}, u32[]{:S(2)}, u32[]{:S(2)}) collective-permute-start(bf16[32,64,128]{2,1,0:T(8,128)(2,1)S(1)} %all-to-all-done), channel_id=1, source_target_pairs={{0,130},{2,128},{128,2},{130,0},{1,131},{3,129},{129,3},{131,1},{4... | collective-permute-start | bytes 1572872 | tf_op jit(solution)/shard_map/ppermute | solution.py:74
  63.9 77.2 %copy-start.11 = (f32[64]{0:T(128)}, f32[64]{0:T(128)S(1)}, u32[]{:S(2)}) copy-start(f32[64]{0:T(128)S(1)} %multiply_power_fusion) | copy-start | bytes 772
  63.9 100.1 %collective-permute-start.6 = (bf16[512,128]{1,0:T(8,128)(2,1)}, bf16[512,128]{1,0:T(8,128)(2,1)}, u32[]{:S(2)}, u32[]{:S(2)}) collective-permute-start(bf16[512,128]{1,0:T(8,128)(2,1)} %bitcast.16), channel_id=1, source_target_pairs={{0,0},{1,2},{2,1},{3,3},{4,4},{5,6},{6,5},{7,7},{8,8},{9,10},{10,9... | collective-permute-start | bytes 393224 | tf_op jit(solution)/shard_map/ppermute | solution.py:69
  73.5 53.9 %collective-permute-start.5 = (bf16[8,128,256]{2,1,0:T(8,128)(2,1)}, bf16[8,128,256]{2,1,0:T(8,128)(2,1)S(1)}, u32[]{:S(2)}, u32[]{:S(2)}) collective-permute-start(bf16[8,128,256]{2,1,0:T(8,128)(2,1)} %all-to-all-done.1), channel_id=1, source_target_pairs={{0,0},{1,2},{2,1},{3,3},{4,4},{5,6},{6,5},{7,7},{8,8},{9,10},{10,9... | collective-permute-start | bytes 1572872 | tf_op jit(solution)/shard_map/ppermute | solution.py:69
  127.5 5.5 %copy-start.4 = (bf16[8,128,256]{2,1,0:T(8,128)(2,1)}, bf16[8,128,256]{2,1,0:T(8,128)(2,1)S(1)}, u32[]{:S(2)}) copy-start(bf16[8,128,256]{2,1,0:T(8,128)(2,1)S(1)} %collective-permute-done.5) | copy-start | bytes 1572868
  128.7 18.8 %all-to-all-start.2 = ((f32[8,64,256]{2,1,0:T(8,128)}), f32[8,64,256]{2,1,0:T(8,128)}, u32[]{:S(2)}, u32[]{:S(2)}) async-start(f32[8,64,256]{2,1,0:T(8,128)} %fusion.50), calls=%async_computation.2 | async-start | bytes 1048576 | tf_op jit(solution)/shard_map/all_to_all | solution.py:78
  150.4 13.0 %all-to-all-start.3 = ((bf16[8,64,256]{2,1,0:T(8,128)(2,1)}), bf16[8,64,256]{2,1,0:T(8,128)(2,1)S(1)}, u32[]{:S(2)}, u32[]{:S(2)}) async-start(bf16[8,64,256]{2,1,0:T(8,128)(2,1)} %broadcast_in_dim.11), calls=%async_computation.3 | async-start | bytes 524288 | tf_op jit(solution)/shard_map/all_to_all | solution.py:78
  163.4 2.1 copy-start.5
  163.4 0.7 copy-start.10
  163.7 1.8 copy-start.2
  165.5 1.0 copy-start.6
  165.5 1.5 copy-start.12
  171.1 1.8 copy-start.3
  198.9 5.3 %copy-start.7 = (f32[512,64]{0,1:T(8,128)S(1)}, f32[512,64]{0,1:T(8,128)}, u32[]{:S(2)}) copy-start(f32[512,64]{0,1:T(8,128)} %get-tuple-element.24) | copy-start | bytes 393220
  200.2 11.9 %all-to-all-start.7 = ((bf16[4,256,256]{2,1,0:T(8,128)(2,1)}), bf16[4,256,256]{2,1,0:T(8,128)(2,1)S(1)}, u32[]{:S(2)}, u32[]{:S(2)}) async-start(bf16[4,256,256]{2,1,0:T(8,128)(2,1)} %bitcast.103), calls=%async_computation.7 | async-start | bytes 1048576 | tf_op jit(solution)/shard_map/all_to_all | solution.py:78
  212.1 28.5 %all-to-all-start.4 = ((bf16[4,2048,128]{2,1,0:T(8,128)(2,1)}), bf16[4,2048,128]{2,1,0:T(8,128)(2,1)}, u32[]{:S(2)}, u32[]{:S(2)}) async-start(bf16[4,2048,128]{2,1,0:T(8,128)(2,1)} %bitcast.18), calls=%async_computation.4 | async-start | bytes 4194304 | tf_op jit(solution)/shard_map/all_to_all | solution.py:78
  260.0 28.9 %all-to-all-start.9 = ((bf16[4,4,256,256]{3,2,1,0:T(8,128)(2,1)}), bf16[4,4,256,256]{3,2,1,0:T(8,128)(2,1)}, u32[]{:S(2)}, u32[]{:S(2)}) async-start(bf16[4,4,256,256]{3,2,1,0:T(8,128)(2,1)} %broadcast_in_dim.15), calls=%async_computation.9 | async-start | bytes 4194304 | tf_op jit(solution)/shard_map/all_to_all | solution.py:78
  289.0 22.9 %collective-permute-start.12 = (bf16[4,4,256,256]{3,2,1,0:T(8,128)(2,1)}, bf16[4,4,256,256]{3,2,1,0:T(8,128)(2,1)}, u32[]{:S(2)}, u32[]{:S(2)}) collective-permute-start(bf16[4,4,256,256]{3,2,1,0:T(8,128)(2,1)} %all-to-all-done.9), channel_id=1, source_target_pairs={{0,1},{1,0},{2,3},{3,2},{4,5},{5,4},{6,7},{7,6},{8,9},{9,8},{10,11... | collective-permute-start | bytes 6291464 | tf_op jit(solution)/shard_map/ppermute | solution.py:74
  292.0 15.5 %collective-permute-start.10 = (bf16[2048,128]{1,0:T(8,128)(2,1)S(1)}, bf16[2048,128]{1,0:T(8,128)(2,1)S(1)}, u32[]{:S(2)}, u32[]{:S(2)}) collective-permute-start(bf16[2048,128]{1,0:T(8,128)(2,1)S(1)} %subtract_convert_fusion), channel_id=1, source_target_pairs={{0,128},{1,130},{2,129},{3,131},{128,0},{129,2},{130,1},{131,3},{4... | collective-permute-start | bytes 1572872 | tf_op jit(solution)/shard_map/ppermute | solution.py:160
  292.8 14.7 %collective-permute-start.8 = (bf16[2048,128]{1,0:T(8,128)(2,1)S(1)}, bf16[2048,128]{1,0:T(8,128)(2,1)S(1)}, u32[]{:S(2)}, u32[]{:S(2)}) collective-permute-start(bf16[2048,128]{1,0:T(8,128)(2,1)S(1)} %subtract_convert_fusion), channel_id=1, source_target_pairs={{0,0},{1,2},{2,1},{3,3},{4,4},{5,6},{6,5},{7,7},{8,8},{9,10},{10,9... | collective-permute-start | bytes 1572872 | tf_op jit(solution)/shard_map/ppermute | solution.py:69
  307.5 1.9 collective-permute-start.11
  307.5 2.7 collective-permute-start.9
  315.3 2.3 copy-start.1
Sparse Core Ops, SparseCore 0:
  17.3 94.5 all-gather.1
where the time goes:
time: 326 us; the launch traced here: 324 us
  waiting for transfers between devices  129 us (40%)
  starting transfers between devices  65.5 us (20%)
  blocking collectives  42.1 us (13%)
  local copies, waits for them, and re-layouts  32.5 us (10%)
  other arithmetic  20.9 us (6%)
  matrix products  20 us (6%)
  between operations  14.5 us (4%)
    all_to_all x7, waiting for transfers between devices, exchange(): return lax.all_to_all(x, axes, split_axis=0, concat_axis=0, tiled=True)  77.5 us
    all_to_all x3, blocking collectives, exchange(): return lax.all_to_all(x, axes, split_axis=0, concat_axis=0, tiled=True)  42.1 us
    all_to_all x7, starting transfers between devices, exchange(): return lax.all_to_all(x, axes, split_axis=0, concat_axis=0, tiled=True)  37.2 us
    all_gather x1, waiting for transfers between devices, local(): normed = lax.all_gather(normed_own, YZ + ('core',), axis=0, tiled=True)  24.6 us
    ppermute x6, starting transfers between devices, swap(): return lax.ppermute(x, ('xl', 'core'), [(0, 0), (1, 2), (2, 1), (3, 3)])  20.1 us
    ppermute x1, waiting for transfers between devices, local(): lax.ppermute(new_q, ('xh', 'xl', 'core'), [(h * 4 + l * 2 + c, (1 - h) *...  12.5 us
    ppermute x6, waiting for transfers between devices, flip(): return lax.ppermute(x, axes, [(i, n - 1 - i) for i in range(n)])  11.6 us
    unnamed x30, local copies, waits for them, and re-layouts  10.7 us
  transfers between devices with their start and end apart: 21, of which 15 were waited for; matrix products, arithmetic and copies ran while one was open for 16% of the time, Pallas kernels for 0%

commit v1 on v0

--- a/solution.py
+++ b/solution.py
@@ -15,6 +15,10 @@
 MEM = ("zl", "core")
 X = ("xh", "xl")
 FS = ("y", "zh", "zl", "xl")
+_treat_array = lambda a0, lane_axis: jnp.concatenate(
+    lax.all_to_all(jnp.stack([a0 for _ in range(lax.psum(1, lane_axis))], axis=0), lane_axis, 0, 0),
+    axis=0,
+)
 
 
 def rotate(field, cosine_table, sine_table):
@@ -107,7 +111,7 @@
     cot = swap(cotangent[0])
     seg_row = swap(seg_ids[0])
     adv_row = swap(advantage[0])
-    normed = lax.all_gather(normed_own, YZ + ("core",), axis=0, tiled=True)
+    normed = _treat_array(normed_own, lane_axis=YZ + ("core",))
     block_len = normed.shape[0]
     wq = w_query.reshape(2, 64, 32, 2, HD)
     wq = lax.dynamic_index_in_dim(wq, xh, 0, keepdims=False)

time: 326 us -> 460 us (1.41)
  waiting for transfers between devices: 129 us -> 261 us
  starting transfers between devices: 65.5 us -> 83.9 us
  local copies, waits for them, and re-layouts: 32.5 us -> 47.1 us
  between operations: 14.5 us -> 1.1 us
  blocking collectives: 42.1 us -> 30 us
  other arithmetic: 20.9 us -> 15.7 us
    all_to_all x0 -> x1, waiting for transfers between devices: none -> 153 us  [lax.all_to_all(jnp.stack([a0 for _ in range(lax.psum(1, lane_axis))], axi...]
    all_gather x1 -> x0, waiting for transfers between devices: 24.6 us -> none  [local(): normed = lax.all_gather(normed_own, YZ + ('core',), axis=0, tiled=True)]
    all_to_all x3 -> x2, blocking collectives: 42.1 us -> 30 us  [exchange(): return lax.all_to_all(x, axes, split_axis=0, concat_axis=0, tiled=True)]
    all_to_all x0 -> x1, starting transfers between devices: none -> 10.2 us  [lax.all_to_all(jnp.stack([a0 for _ in range(lax.psum(1, lane_axis))], axi...]
    dynamic_slice x1 -> x2, local copies, waits for them, and re-layouts: 5.59 us -> 14.9 us  [local(): lax.dynamic_index_in_dim(normed.reshape(block_len, 8, 8, HD), member, 2,...]
    all_to_all x7 -> x8, starting transfers between devices: 37.2 us -> 45 us  [exchange(): return lax.all_to_all(x, axes, split_axis=0, concat_axis=0, tiled=True)]
    all_to_all x7 -> x8, waiting for transfers between devices: 77.5 us -> 77.3 us  [exchange(): return lax.all_to_all(x, axes, split_axis=0, concat_axis=0, tiled=True)]
    unnamed x30 -> x23, local copies, waits for them, and re-layouts: 10.7 us -> 10.9 us
  transfers between devices with their start and end apart: 21 -> 22, of which waited for: 15 -> 16; matrix products, arithmetic and copies ran while one was open for 16% -> 13% of each run, Pallas kernels for 0% -> 0%
where the time goes in v1:
time: 460 us; the launch traced here: 458 us
  waiting for transfers between devices  261 us (57%)
  starting transfers between devices  83.9 us (18%)
  local copies, waits for them, and re-layouts  47.1 us (10%)
  blocking collectives  30 us (7%)
  matrix products  19.6 us (4%)
  other arithmetic  15.7 us (3%)
    all_to_all x1, waiting for transfers between devices, lax.all_to_all(jnp.stack([a0 for _ in range(lax.psum(1, lane_axis))], axi...  153 us
    all_to_all x8, waiting for transfers between devices, exchange(): return lax.all_to_all(x, axes, split_axis=0, concat_axis=0, tiled=True)  77.3 us
    all_to_all x8, starting transfers between devices, exchange(): return lax.all_to_all(x, axes, split_axis=0, concat_axis=0, tiled=True)  45 us
    all_to_all x2, blocking collectives, exchange(): return lax.all_to_all(x, axes, split_axis=0, concat_axis=0, tiled=True)  30 us
    ppermute x6, starting transfers between devices, swap(): return lax.ppermute(x, ('xl', 'core'), [(0, 0), (1, 2), (2, 1), (3, 3)])  20.5 us
    ppermute x6, waiting for transfers between devices, flip(): return lax.ppermute(x, axes, [(i, n - 1 - i) for i in range(n)])  15.5 us
    dynamic_slice x2, local copies, waits for them, and re-layouts, local(): lax.dynamic_index_in_dim(normed.reshape(block_len, 8, 8, HD), member, 2,...  14.9 us
    ppermute x1, waiting for transfers between devices, local(): lax.ppermute(new_q, ('xh', 'xl', 'core'), [(h * 4 + l * 2 + c, (1 - h) *...  12.5 us
  transfers between devices with their start and end apart: 22, of which 16 were waited for; matrix products, arithmetic and copies ran while one was open for 13% of the time, Pallas kernels for 0%

profile of v1, /device:TPU:1, one launch (start us, length us, event | category | flops | bytes accessed | tf_op | source)
XLA Modules:
  0.0 458.4 jit_solution(11540778766408248653)
XLA Ops:
  3.5 11.6 %all-to-all-start.2 = ((bf16[8,128,256]{2,1,0:T(8,128)(2,1)}), bf16[8,128,256]{2,1,0:T(8,128)(2,1)}, u32[]{:S(2)}, u32[]{:S(2)}) async-start(bf16[8,128,256]{2,1,0:T(8,128)(2,1)} %maximum_bitcast_fusion.1), calls=%async_computation.2 | async-start | bytes 1048576 | tf_op jit(solution)/shard_map/all_to_all | solution.py:82
  15.2 3.2 reshape.129
  19.6 1.4 copy.65
  21.2 8.2 %all-to-all-done.2 = bf16[8,128,256]{2,1,0:T(8,128)(2,1)} async-done(((bf16[8,128,256]{2,1,0:T(8,128)(2,1)}), bf16[8,128,256]{2,1,0:T(8,128)(2,1)}, u32[]{:S(2)}, u32[]{:S(2)}) %all-to-all-start.2) | async-done | bytes 524320 | tf_op jit(solution)/shard_map/all_to_all | solution.py:82
  29.4 8.2 %all-to-all-start = ((bf16[32,64,128]{2,1,0:T(8,128)(2,1)}), bf16[32,64,128]{2,1,0:T(8,128)(2,1)S(1)}, u32[]{:S(2)}, u32[]{:S(2)}) async-start(bf16[32,64,128]{2,1,0:T(8,128)(2,1)} %bitcast.85), calls=%async_computation | async-start | bytes 1048576 | tf_op jit(solution)/shard_map/all_to_all | solution.py:82
  37.7 4.7 %collective-permute-start.3 = (bf16[8,8192]{1,0:T(8,128)(2,1)S(1)}, bf16[8,8192]{1,0:T(8,128)(2,1)S(1)}, u32[]{:S(2)}, u32[]{:S(2)}) collective-permute-start(bf16[8,8192]{1,0:T(8,128)(2,1)S(1)} %fusion.15), channel_id=1, source_target_pairs={{0,0},{1,2},{2,1},{3,3},{4,4},{5,6},{6,5},{7,7},{8,8},{9,10},{10,9... | collective-permute-start | bytes 393224 | tf_op jit(solution)/shard_map/ppermute | solution.py:73
  42.4 2.9 collective-permute-done.3
  45.3 6.0 %all-to-all-done = bf16[32,64,128]{2,1,0:T(8,128)(2,1)S(1)} async-done(((bf16[32,64,128]{2,1,0:T(8,128)(2,1)}), bf16[32,64,128]{2,1,0:T(8,128)(2,1)S(1)}, u32[]{:S(2)}, u32[]{:S(2)}) %all-to-all-start) | async-done | bytes 524320 | tf_op jit(solution)/shard_map/all_to_all | solution.py:82
  51.3 4.3 stack.33
  55.6 10.2 %all-to-all-start.1 = ((bf16[64,8,8192]{2,1,0:T(8,128)(2,1)}), bf16[64,8,8192]{2,1,0:T(8,128)(2,1)}, u32[]{:S(2)}, u32[]{:S(2)}) async-start(bf16[64,8,8192]{2,1,0:T(8,128)(2,1)} %stack.33), calls=%async_computation.1 | async-start | bytes 16777216 | tf_op jit(solution)/shard_map/all_to_all | solution.py:19
  65.8 3.5 collective-permute-start.4
  69.3 2.0 collective-permute-start.7
  71.5 2.8 collective-permute-start.1
  75.4 3.2 collective-permute-start.6
  78.9 6.2 %collective-permute-done = bf16[32,64,128]{2,1,0:T(8,128)(2,1)S(1)} collective-permute-done((bf16[32,64,128]{2,1,0:T(8,128)(2,1)S(1)}, bf16[32,64,128]{2,1,0:T(8,128)(2,1)S(1)}, u32[]{:S(2)}, u32[]{:S(2)}) %collective-permute-start) | collective-permute-done | bytes 524320 | tf_op jit(solution)/shard_map/ppermute | solution.py:78
  85.0 4.9 %collective-permute-start.5 = (bf16[8,128,256]{2,1,0:T(8,128)(2,1)}, bf16[8,128,256]{2,1,0:T(8,128)(2,1)S(1)}, u32[]{:S(2)}, u32[]{:S(2)}) collective-permute-start(bf16[8,128,256]{2,1,0:T(8,128)(2,1)} %all-to-all-done.2), channel_id=1, source_target_pairs={{0,0},{1,2},{2,1},{3,3},{4,4},{5,6},{6,5},{7,7},{8,8},{9,10},{10,9... | collective-permute-start | bytes 1572872 | tf_op jit(solution)/shard_map/ppermute | solution.py:73
  90.0 6.3 %collective-permute-done.1 = bf16[32,64,128]{2,1,0:T(8,128)(2,1)S(1)} collective-permute-done((bf16[32,64,128]{2,1,0:T(8,128)(2,1)S(1)}, bf16[32,64,128]{2,1,0:T(8,128)(2,1)S(1)}, u32[]{:S(2)}, u32[]{:S(2)}) %collective-permute-start.1) | collective-permute-done | bytes 524320 | tf_op jit(solution)/shard_map/ppermute | solution.py:78
  97.2 1.5 select_bitcast_fusion.7
  98.6 152.9 %all-to-all-done.1 = bf16[64,8,8192]{2,1,0:T(8,128)(2,1)} async-done(((bf16[64,8,8192]{2,1,0:T(8,128)(2,1)}), bf16[64,8,8192]{2,1,0:T(8,128)(2,1)}, u32[]{:S(2)}, u32[]{:S(2)}) %all-to-all-start.1) | async-done | bytes 8388640 | tf_op jit(solution)/shard_map/all_to_all | solution.py:19
  251.5 9.3 %copy.61 = bf16[64,8,64,128]{3,2,1,0:T(8,128)(2,1)} copy(bf16[64,8,64,128]{3,1,2,0:T(8,128)(2,1)} %bitcast.49) | data formatting | bytes 16777216
  260.9 10.3 %fusion.53 = (bf16[512,8,128]{2,1,0:T(8,128)(2,1)S(1)}, bf16[512,8,1,128]{3,2,1,0:T(2,128)(2,1)}) fusion(bf16[512,8,8,128]{3,2,1,0:T(8,128)(2,1)} %bitcast.87, s32[]{:T(128)S(6)} %select_n.135), kind=kLoop, calls=%fused_computation.110 | loop fusion | bytes 3145732 | tf_op jit(solution)/shard_map/jit(dynamic_index_in_dim)/dynamic_slice | solution.py:135
  273.0 3.7 all-to-all-start.3
  276.6 1.6 pad_maximum_fusion
  278.3 6.3 %fusion.3 = f32[512,128]{0,1:T(8,128)S(1)} fusion(bf16[8192,128]{1,0:T(8,128)(2,1)S(1)} %bitcast.88, bf16[64,8,8192]{2,1,0:T(8,128)(2,1)} %all-to-all-done.1), kind=kOutput, calls=%fused_computation.14 | convolution fusion | flops 1073807360 | bytes 10747904 | tf_op jit(solution)/shard_map/dot_general | solution.py:146
  285.1 5.2 %all-to-all-done.3 = f32[8,64,256]{2,1,0:T(8,128)S(1)} async-done(((f32[8,64,256]{2,1,0:T(8,128)}), f32[8,64,256]{2,1,0:T(8,128)S(1)}, u32[]{:S(2)}, u32[]{:S(2)}) %all-to-all-start.3) | async-done | bytes 524320 | tf_op jit(solution)/shard_map/all_to_all | solution.py:82
  291.4 4.3 all-to-all-start.4
  297.0 7.4 %all-to-all-done.4 = bf16[8,64,256]{2,1,0:T(8,128)(2,1)S(1)} async-done(((bf16[8,64,256]{2,1,0:T(8,128)(2,1)}), bf16[8,64,256]{2,1,0:T(8,128)(2,1)S(1)}, u32[]{:S(2)}, u32[]{:S(2)}) %all-to-all-start.4) | async-done | bytes 262176 | tf_op jit(solution)/shard_map/all_to_all | solution.py:82
  310.4 1.7 copy.56
  312.1 1.4 fusion.12
  313.8 12.1 %all_to_all.55 = bf16[8,64,256]{2,1,0:T(8,128)(2,1)S(1)} all-to-all(bf16[8,64,256]{2,1,0:T(8,128)(2,1)S(1)} %fusion.11), channel_id=1, replica_groups=mesh['xh'=2,'y'=4,'zh'=2,'zl'=4,'xl'=2,'core'=2] {'zl','core'}, dimensions={0} | all-to-all | bytes 524288 | tf_op jit(solution)/shard_map/all_to_all | solution.py:82
  326.7 4.4 all-to-all-start.7
  331.0 4.6 copy.51
  335.6 4.1 all-to-all-done.7
  341.0 4.0 all-to-all-start.8
  345.0 7.1 %convolution_convert_fusion = bf16[8192,128]{1,0:T(8,128)(2,1)} fusion(bf16[64,8,8192]{2,1,0:T(8,128)(2,1)} %all-to-all-done.1, f32[512,64]{0,1:T(8,128)S(1)} %get-tuple-element.25, f32[512,64]{0,1:T(8,128)} %get-tuple-element.26), kind=kOutput, calls=%fused_computation | convolution fusion | flops 1074987008 | bytes 10747904 | tf_op jit(solution)/shard_map/dot_general | solution.py:159
  352.9 4.4 all-to-all-start.5
  358.4 23.0 %all-to-all-done.5 = bf16[4,2048,128]{2,1,0:T(8,128)(2,1)} async-done(((bf16[4,2048,128]{2,1,0:T(8,128)(2,1)}), bf16[4,2048,128]{2,1,0:T(8,128)(2,1)}, u32[]{:S(2)}, u32[]{:S(2)}) %all-to-all-start.5) | async-done | bytes 2097184 | tf_op jit(solution)/shard_map/all_to_all | solution.py:82
  381.4 17.8 %all_to_all.56 = bf16[4,256,256]{2,1,0:T(8,128)(2,1)S(1)} all-to-all(bf16[4,256,256]{2,1,0:T(8,128)(2,1)S(1)} %broadcast_in_dim.14), channel_id=1, replica_groups=mesh['xh'=2,'y'=4,'zh'=2,'zl'=4,'xl'=2,'core'=2] {'zl'}, dimensions={0} | all-to-all | bytes 1048576 | tf_op jit(solution)/shard_map/all_to_all | solution.py:82
  399.3 1.5 broadcast_in_dim.15
  400.8 4.5 all-to-all-start.10
  405.3 2.0 convert_reduce_fusion
  407.3 22.5 %all-to-all-done.10 = bf16[4,4,256,256]{3,2,1,0:T(8,128)(2,1)} async-done(((bf16[4,4,256,256]{3,2,1,0:T(8,128)(2,1)}), bf16[4,4,256,256]{3,2,1,0:T(8,128)(2,1)}, u32[]{:S(2)}, u32[]{:S(2)}) %all-to-all-start.10) | async-done | bytes 2097184 | tf_op jit(solution)/shard_map/all_to_all | solution.py:82
  429.8 2.9 collective-permute-start.12
  433.6 2.2 collective-permute-start.8
  435.8 12.5 %collective-permute-done.10 = bf16[2048,128]{1,0:T(8,128)(2,1)S(1)} collective-permute-done((bf16[2048,128]{1,0:T(8,128)(2,1)S(1)}, bf16[2048,128]{1,0:T(8,128)(2,1)S(1)}, u32[]{:S(2)}, u32[]{:S(2)}) %collective-permute-start.10) | collective-permute-done | bytes 524320 | tf_op jit(solution)/shard_map/ppermute | solution.py:164
  451.1 1.6 pad_maximum_fusion.1
  452.7 2.5 broadcast_select_fusion.1
  456.1 2.3 fusion.54
  (81 shorter events, 26.2 us)
Async XLA Ops:
  0.6 1.0 copy-start
  3.5 25.9 %all-to-all-start.2 = ((bf16[8,128,256]{2,1,0:T(8,128)(2,1)}), bf16[8,128,256]{2,1,0:T(8,128)(2,1)}, u32[]{:S(2)}, u32[]{:S(2)}) async-start(bf16[8,128,256]{2,1,0:T(8,128)(2,1)} %maximum_bitcast_fusion.1), calls=%async_computation.2 | async-start | bytes 1048576 | tf_op jit(solution)/shard_map/all_to_all | solution.py:82
  18.4 2.7 copy-start.6
  29.4 21.9 %all-to-all-start = ((bf16[32,64,128]{2,1,0:T(8,128)(2,1)}), bf16[32,64,128]{2,1,0:T(8,128)(2,1)S(1)}, u32[]{:S(2)}, u32[]{:S(2)}) async-start(bf16[32,64,128]{2,1,0:T(8,128)(2,1)} %bitcast.85), calls=%async_computation | async-start | bytes 1048576 | tf_op jit(solution)/shard_map/all_to_all | solution.py:82
  37.7 7.6 %collective-permute-start.3 = (bf16[8,8192]{1,0:T(8,128)(2,1)S(1)}, bf16[8,8192]{1,0:T(8,128)(2,1)S(1)}, u32[]{:S(2)}, u32[]{:S(2)}) collective-permute-start(bf16[8,8192]{1,0:T(8,128)(2,1)S(1)} %fusion.15), channel_id=1, source_target_pairs={{0,0},{1,2},{2,1},{3,3},{4,4},{5,6},{6,5},{7,7},{8,8},{9,10},{10,9... | collective-permute-start | bytes 393224 | tf_op jit(solution)/shard_map/ppermute | solution.py:73
  55.6 10.2 %copy-start.10 = (s32[1,512]{1,0:T(1,128)S(1)}, s32[1,512]{1,0:T(1,128)}, u32[]{:S(2)}) copy-start(s32[1,512]{1,0:T(1,128)} %param.9) | copy-start | bytes 6148
  55.6 195.9 %all-to-all-start.1 = ((bf16[64,8,8192]{2,1,0:T(8,128)(2,1)}), bf16[64,8,8192]{2,1,0:T(8,128)(2,1)}, u32[]{:S(2)}, u32[]{:S(2)}) async-start(bf16[64,8,8192]{2,1,0:T(8,128)(2,1)} %stack.33), calls=%async_computation.1 | async-start | bytes 16777216 | tf_op jit(solution)/shard_map/all_to_all | solution.py:19
  65.8 9.6 %collective-permute-start.4 = (s32[512]{0:T(512)S(1)}, s32[512]{0:T(512)S(1)}, u32[]{:S(2)}, u32[]{:S(2)}) collective-permute-start(s32[512]{0:T(512)S(1)} %bitcast.103), channel_id=1, source_target_pairs={{0,0},{1,2},{2,1},{3,3},{4,4},{5,6},{6,5},{7,7},{8,8},{9,10},{10,9... | collective-permute-start | bytes 6152 | tf_op jit(solution)/shard_map/ppermute | solution.py:73
  69.3 226.4 %collective-permute-start.7 = (f32[8]{0:T(128)}, f32[8]{0:T(128)}, u32[]{:S(2)}, u32[]{:S(2)}) collective-permute-start(f32[8]{0:T(128)} %bitcast.18), channel_id=1, source_target_pairs={{0,0},{1,2},{2,1},{3,3},{4,4},{5,6},{6,5},{7,7},{8,8},{9,10},{10,9... | collective-permute-start | bytes 104 | tf_op jit(solution)/shard_map/ppermute | solution.py:73
  71.4 13.7 %collective-permute-start = (bf16[32,64,128]{2,1,0:T(8,128)(2,1)S(1)}, bf16[32,64,128]{2,1,0:T(8,128)(2,1)S(1)}, u32[]{:S(2)}, u32[]{:S(2)}) collective-permute-start(bf16[32,64,128]{2,1,0:T(8,128)(2,1)S(1)} %all-to-all-done), channel_id=1, source_target_pairs={{0,2},{2,0},{1,3},{3,1},{4,6},{6,4},{5,7},{7,5},{8,10},{10,8},{9,1... | collective-permute-start | bytes 1572872 | tf_op jit(solution)/shard_map/ppermute | solution.py:78
  71.5 24.8 %collective-permute-start.1 = (bf16[32,64,128]{2,1,0:T(8,128)(2,1)S(1)}, bf16[32,64,128]{2,1,0:T(8,128)(2,1)S(1)}, u32[]{:S(2)}, u32[]{:S(2)}) collective-permute-start(bf16[32,64,128]{2,1,0:T(8,128)(2,1)S(1)} %all-to-all-done), channel_id=1, source_target_pairs={{0,128},{128,0},{1,129},{129,1},{2,130},{130,2},{3,131},{131,3},{4... | collective-permute-start | bytes 1572872 | tf_op jit(solution)/shard_map/ppermute | solution.py:78
  74.3 22.9 %collective-permute-start.2 = (bf16[32,64,128]{2,1,0:T(8,128)(2,1)S(1)}, bf16[32,64,128]{2,1,0:T(8,128)(2,1)S(1)}, u32[]{:S(2)}, u32[]{:S(2)}) collective-permute-start(bf16[32,64,128]{2,1,0:T(8,128)(2,1)S(1)} %all-to-all-done), channel_id=1, source_target_pairs={{0,130},{2,128},{128,2},{130,0},{1,131},{3,129},{129,3},{131,1},{4... | collective-permute-start | bytes 1572872 | tf_op jit(solution)/shard_map/ppermute | solution.py:78
  75.3 209.2 %copy-start.8 = (f32[64]{0:T(128)}, f32[64]{0:T(128)S(1)}, u32[]{:S(2)}) copy-start(f32[64]{0:T(128)S(1)} %multiply_power_fusion) | copy-start | bytes 772
  75.4 229.7 %collective-permute-start.6 = (bf16[512,128]{1,0:T(8,128)(2,1)}, bf16[512,128]{1,0:T(8,128)(2,1)}, u32[]{:S(2)}, u32[]{:S(2)}) collective-permute-start(bf16[512,128]{1,0:T(8,128)(2,1)} %bitcast.17), channel_id=1, source_target_pairs={{0,0},{1,2},{2,1},{3,3},{4,4},{5,6},{6,5},{7,7},{8,8},{9,10},{10,9... | collective-permute-start | bytes 393224 | tf_op jit(solution)/shard_map/ppermute | solution.py:73
  85.0 186.7 %collective-permute-start.5 = (bf16[8,128,256]{2,1,0:T(8,128)(2,1)}, bf16[8,128,256]{2,1,0:T(8,128)(2,1)S(1)}, u32[]{:S(2)}, u32[]{:S(2)}) collective-permute-start(bf16[8,128,256]{2,1,0:T(8,128)(2,1)} %all-to-all-done.2), channel_id=1, source_target_pairs={{0,0},{1,2},{2,1},{3,3},{4,4},{5,6},{6,5},{7,7},{8,8},{9,10},{10,9... | collective-permute-start | bytes 1572872 | tf_op jit(solution)/shard_map/ppermute | solution.py:73
  271.7 1.3 copy-start.3
  273.0 17.4 %all-to-all-start.3 = ((f32[8,64,256]{2,1,0:T(8,128)}), f32[8,64,256]{2,1,0:T(8,128)S(1)}, u32[]{:S(2)}, u32[]{:S(2)}) async-start(f32[8,64,256]{2,1,0:T(8,128)} %fusion.55), calls=%async_computation.3 | async-start | bytes 1048576 | tf_op jit(solution)/shard_map/all_to_all | solution.py:82
  291.4 13.0 %all-to-all-start.4 = ((bf16[8,64,256]{2,1,0:T(8,128)(2,1)}), bf16[8,64,256]{2,1,0:T(8,128)(2,1)S(1)}, u32[]{:S(2)}, u32[]{:S(2)}) async-start(bf16[8,64,256]{2,1,0:T(8,128)(2,1)} %broadcast_in_dim.11), calls=%async_computation.4 | async-start | bytes 524288 | tf_op jit(solution)/shard_map/all_to_all | solution.py:82
  304.4 2.1 copy-start.4
  304.4 0.7 copy-start.7
  306.5 1.0 copy-start.5
  306.5 1.5 copy-start.9
  312.1 1.4 copy-start.2
  326.7 13.1 %all-to-all-start.7 = ((bf16[8,64,256]{2,1,0:T(8,128)(2,1)}), bf16[8,64,256]{2,1,0:T(8,128)(2,1)S(1)}, u32[]{:S(2)}, u32[]{:S(2)}) async-start(bf16[8,64,256]{2,1,0:T(8,128)(2,1)} %broadcast_in_dim.13), calls=%async_computation.7 | async-start | bytes 524288 | tf_op jit(solution)/shard_map/all_to_all | solution.py:82
  341.0 12.0 %all-to-all-start.8 = ((bf16[4,256,256]{2,1,0:T(8,128)(2,1)}), bf16[4,256,256]{2,1,0:T(8,128)(2,1)S(1)}, u32[]{:S(2)}, u32[]{:S(2)}) async-start(bf16[4,256,256]{2,1,0:T(8,128)(2,1)} %bitcast.93), calls=%async_computation.8 | async-start | bytes 1048576 | tf_op jit(solution)/shard_map/all_to_all | solution.py:82
  352.9 28.5 %all-to-all-start.5 = ((bf16[4,2048,128]{2,1,0:T(8,128)(2,1)}), bf16[4,2048,128]{2,1,0:T(8,128)(2,1)}, u32[]{:S(2)}, u32[]{:S(2)}) async-start(bf16[4,2048,128]{2,1,0:T(8,128)(2,1)} %bitcast.19), calls=%async_computation.5 | async-start | bytes 4194304 | tf_op jit(solution)/shard_map/all_to_all | solution.py:82
  400.8 29.0 %all-to-all-start.10 = ((bf16[4,4,256,256]{3,2,1,0:T(8,128)(2,1)}), bf16[4,4,256,256]{3,2,1,0:T(8,128)(2,1)}, u32[]{:S(2)}, u32[]{:S(2)}) async-start(bf16[4,4,256,256]{3,2,1,0:T(8,128)(2,1)} %broadcast_in_dim.15), calls=%async_computation.10 | async-start | bytes 4194304 | tf_op jit(solution)/shard_map/all_to_all | solution.py:82
  429.8 22.9 %collective-permute-start.12 = (bf16[4,4,256,256]{3,2,1,0:T(8,128)(2,1)}, bf16[4,4,256,256]{3,2,1,0:T(8,128)(2,1)}, u32[]{:S(2)}, u32[]{:S(2)}) collective-permute-start(bf16[4,4,256,256]{3,2,1,0:T(8,128)(2,1)} %all-to-all-done.10), channel_id=1, source_target_pairs={{0,1},{1,0},{2,3},{3,2},{4,5},{5,4},{6,7},{7,6},{8,9},{9,8},{10,11... | collective-permute-start | bytes 6291464 | tf_op jit(solution)/shard_map/ppermute | solution.py:78
  432.8 15.5 %collective-permute-start.10 = (bf16[2048,128]{1,0:T(8,128)(2,1)S(1)}, bf16[2048,128]{1,0:T(8,128)(2,1)S(1)}, u32[]{:S(2)}, u32[]{:S(2)}) collective-permute-start(bf16[2048,128]{1,0:T(8,128)(2,1)S(1)} %subtract_convert_fusion), channel_id=1, source_target_pairs={{0,128},{1,130},{2,129},{3,131},{128,0},{129,2},{130,1},{131,3},{4... | collective-permute-start | bytes 1572872 | tf_op jit(solution)/shard_map/ppermute | solution.py:164
  433.6 14.7 %collective-permute-start.8 = (bf16[2048,128]{1,0:T(8,128)(2,1)S(1)}, bf16[2048,128]{1,0:T(8,128)(2,1)S(1)}, u32[]{:S(2)}, u32[]{:S(2)}) collective-permute-start(bf16[2048,128]{1,0:T(8,128)(2,1)S(1)} %subtract_convert_fusion), channel_id=1, source_target_pairs={{0,0},{1,2},{2,1},{3,3},{4,4},{5,6},{6,5},{7,7},{8,8},{9,10},{10,9... | collective-permute-start | bytes 1572872 | tf_op jit(solution)/shard_map/ppermute | solution.py:73
  448.3 1.9 collective-permute-start.11
  448.3 2.7 collective-permute-start.9
  456.1 2.3 copy-start.1
